TPU v7x, 256 devices: a whole 4x4x8 slice. The times are simulated.
256 devices in a mesh: lon: 16 (over y, z_lo, core), lat: 16 (over x, z_hi).
Axes of the slice: x: 4, y: 4, z: 8 (z_hi: 4, z_lo: 2; z = z_hi * 2 + z_lo), core: 2. Of those that a mesh axis runs over, the one named last changes fastest.
Arguments:
- fine_state: bfloat16 [2048, 1024, 128], P('lon', 'lat'), may hold values from -6 to 6
- coarse_state: bfloat16 [128, 64, 512], P('lon', 'lat'), may hold values from -6 to 6
- norm_gains: float32 [2, 128], replicated, may hold values from 0.25 to 1.75
- kernels: bfloat16 [2, 3, 3, 128, 128], replicated, may hold values from -0.1875 to 0.1875
- token_gain: float32 [512], replicated, may hold values from 0.25 to 1.75
- head_gains: float32 [2, 64], replicated, may hold values from 1.2 to 2.2
- query_weight: bfloat16 [512, 512], replicated, may hold values from -0.25 to 0.25
- keyvalue_weight: bfloat16 [512, 1024], replicated, may hold values from -0.25 to 0.25
- output_weight: bfloat16 [512, 512], replicated, may hold values from -0.25 to 0.25
- expand_weight: bfloat16 [512, 128], replicated, may hold values from -0.25 to 0.25
Outputs:
- fine_result: bfloat16 [2048, 1024, 128], P('lon', 'lat')
- coarse_result: bfloat16 [128, 64, 512], P('lon', 'lat')
All inputs are finite; a program needn't handle non-finite values.
Results may differ from a plain program's by a relative error of at most 0.005.
Values may be sent and summed in bfloat16 or wider, within the bound.
No kernel may reach another device: no remote copies, remote signals or barrier semaphores. Data moves between devices by JAX's collectives and lax.ppermute only.
A program may use at most 192 MiB of HBM per device.

v0:
```python
import math
import jax
import jax.numpy as jnp
from jax import lax
from jax.sharding import PartitionSpec as P


def padded_2(block, sides, width, periodic):
    for axis, dim in sides:
        count = lax.axis_size(axis)
        forward = [(i, i + 1) for i in range(count - 1)]
        if periodic:
            forward.append((count - 1, 0))
        backward = [(target, source) for source, target in forward]
        low = lax.ppermute(
            lax.slice_in_dim(block, block.shape[dim] - width, None, axis=dim), axis, forward
        )
        high = lax.ppermute(lax.slice_in_dim(block, 0, width, axis=dim), axis, backward)
        block = jnp.concatenate([low, block, high], axis=dim)
    return block


def rescale_rows(matrix, gain_row):
    return matrix * lax.rsqrt(jnp.mean(matrix * matrix, axis=-1, keepdims=True) + 1e-06) * gain_row


def rescale_heads(projected, gain_row):
    shaped = projected.reshape(projected.shape[0], -1, gain_row.shape[0])
    return rescale_rows(shaped, gain_row)


def convolve(padded, kernel):
    return lax.conv_general_dilated(
        padded[None],
        kernel,
        (1, 1),
        "VALID",
        dimension_numbers=("NHWC", "HWIO", "NHWC"),
        preferred_element_type=jnp.float32,
    )[0]


def attach_rims(hidden, rim_width):
    wrapped = padded_2(hidden, (("lon", 0),), rim_width, True)
    return padded_2(wrapped, (("lat", 1),), rim_width, False)


def local(
    fine_state,
    coarse_state,
    norm_gains,
    kernels,
    token_gain,
    head_gains,
    query_weight,
    keyvalue_weight,
    output_weight,
    expand_weight,
):
    width_all = query_weight.shape[0]
    head_size = head_gains.shape[1]
    head_count = width_all // head_size
    lon_tokens = coarse_state.shape[0]
    lat_tokens = coarse_state.shape[1]
    lon_cells, lat_cells, channels = fine_state.shape
    first_hidden = jax.nn.silu(rescale_rows(fine_state.astype(jnp.float32), norm_gains[0])).astype(
        jnp.bfloat16
    )
    first_output = convolve(attach_rims(first_hidden, 1), kernels[0])
    second_hidden = jax.nn.silu(rescale_rows(first_output, norm_gains[1])).astype(jnp.bfloat16)
    second_output = convolve(attach_rims(second_hidden, 1), kernels[1])
    tokens = coarse_state.reshape(-1, width_all)
    normed = rescale_rows(tokens.astype(jnp.float32), token_gain).astype(jnp.bfloat16)
    scale_factor = 1.0 / math.sqrt(head_size)
    queries = (
        rescale_heads(
            jnp.dot(normed, query_weight, preferred_element_type=jnp.float32), head_gains[0]
        )
        * scale_factor
    ).astype(jnp.bfloat16)
    projected = jnp.dot(normed, keyvalue_weight, preferred_element_type=jnp.float32)
    key_rows = (
        rescale_heads(projected[:, :width_all], head_gains[1])
        .astype(jnp.bfloat16)
        .reshape(-1, width_all)
    )
    value_rows = projected[:, width_all:].astype(jnp.bfloat16)
    key_rows, value_rows = (key_rows, value_rows)
    accumulate_key_rows = lax.all_gather(key_rows, ("lon", "lat"), axis=0, tiled=True)
    accumulate_value_rows = lax.all_gather(value_rows, ("lon", "lat"), axis=0, tiled=True)
    key_heads = accumulate_key_rows.reshape(accumulate_key_rows.shape[0], head_count, head_size)
    value_heads = accumulate_value_rows.reshape(
        accumulate_value_rows.shape[0], head_count, head_size
    )
    scores = jnp.einsum("thd,shd->hts", queries, key_heads, preferred_element_type=jnp.float32)
    weights = jnp.exp(scores)
    totals = jnp.sum(weights, axis=-1)
    summed = jnp.einsum(
        "hts,shd->thd",
        weights.astype(jnp.bfloat16),
        value_heads,
        preferred_element_type=jnp.float32,
    )
    summed, totals = (summed, totals)
    attended = (
        (summed / jnp.transpose(totals)[:, :, None]).reshape(-1, width_all).astype(jnp.bfloat16)
    )
    coarse_result = (
        tokens.astype(jnp.float32)
        + jnp.dot(attended, output_weight, preferred_element_type=jnp.float32)
    ).astype(jnp.bfloat16)
    lifted = jnp.dot(coarse_result, expand_weight, preferred_element_type=jnp.float32).reshape(
        lon_tokens, 1, lat_tokens, 1, channels
    )
    merged = (fine_state.astype(jnp.float32) + second_output).reshape(
        lon_tokens, lon_cells // lon_tokens, lat_tokens, lat_cells // lat_tokens, channels
    ) + lifted
    fine_result = merged.reshape(lon_cells, lat_cells, channels).astype(jnp.bfloat16)
    return (fine_result, coarse_result.reshape(lon_tokens, lat_tokens, width_all))


def solution(mesh):
    return jax.shard_map(
        local,
        mesh=mesh,
        in_specs=(
            P("lon", "lat", None),
            P("lon", "lat", None),
            P(),
            P(),
            P(),
            P(),
            P(),
            P(),
            P(),
            P(),
        ),
        out_specs=(P("lon", "lat", None), P("lon", "lat", None)),
        check_vma=False,
    )
```

profile of v0, /device:TPU:99, one launch (start us, length us, event | category | flops | bytes accessed | tf_op | source)
XLA Modules:
  0.0 1499.1 jit_solution(16317238744384808810)
XLA Ops:
  7.2 0.8 reshape.112
  8.1 0.9 multiply_reduce_fusion.2
  9.0 1.0 fusion.51
  10.6 0.8 slice_bitcast_fusion.3
  11.4 0.6 multiply_convert_fusion.3
  12.2 0.6 slice.102
  12.9 0.8 slice_bitcast_fusion.4
  13.6 3.4 fusion.2
  17.1 3.4 fusion.9
  20.6 0.8 collective-permute-start.1
  21.3 2.0 collective-permute-start
  23.3 1.8 collective-permute-done.1
  25.1 1.9 collective-permute-start.3
  27.0 5.7 collective-permute-start.2
  32.8 0.2 copy.52
  33.1 1.6 collective-permute-done.2
  34.7 1.7 maximum_bitcast_fusion
  36.4 0.2 pad
  36.6 0.3 copy.46
  37.1 0.4 copy-done.8
  37.5 5.7 broadcast_select_fusion.1
  43.2 0.9 copy.47
  44.1 1.2 multiply_reduce_fusion
  45.3 1.5 multiply_convert_fusion
  46.8 1.6 collective-permute-start.5
  48.4 2.2 collective-permute-start.4
  50.6 0.4 multiply_reduce_fusion.1
  51.1 1.2 collective-permute-done.5
  52.4 6.7 collective-permute-start.7
  59.0 2.1 collective-permute-start.6
  61.2 3.5 collective-permute-done.6
  64.7 1.8 maximum_bitcast_fusion.1
  66.5 0.2 pad.2
  66.7 0.3 copy.49
  67.0 0.1 slice.75
  67.1 5.7 broadcast_select_fusion
  72.8 3.0 copy.50
  75.8 665.4 %all-gather.5.cloned.1.call-done = bf16[8192,512]{1,0:T(8,128)(2,1)} async-done(((bf16[32,512]{1,0:T(8,128)(2,1)}), bf16[8192,512]{1,0:T(8,128)(2,1)}) %all-gather.5.cloned.1.call-update) | async-done | bytes 8388624 | tf_op jit(solution)/shard_map/all_gather | solution.py:89
  741.2 12.0 copy.55
  753.2 7.0 fusion.63
  760.2 705.3 %all-gather.3.cloned.1.call-done = bf16[8192,512]{1,0:T(8,128)(2,1)} async-done(((bf16[32,512]{1,0:T(8,128)(2,1)}), bf16[8192,512]{1,0:T(8,128)(2,1)}) %all-gather.3.cloned.1.call-update) | async-done | bytes 8388624 | tf_op jit(solution)/shard_map/all_gather | solution.py:90
  1465.4 11.6 copy.51
  1477.0 6.9 fusion.41
  1484.1 0.2 fusion.37
  1484.3 0.6 reshape.97
  1485.1 0.5 add.82
  1485.6 4.0 fusion.11
  1489.6 2.7 copy.58
  (53 shorter events, 1.7 us)
Async XLA Ops:
  7.2 1.9 copy-start
  7.2 734.0 %all-gather.5.cloned.1.call-start = ((), (), s32[]{:S(2)}) async-start(), calls=%async_computation.1 | async-start | bytes 8421376 | tf_op jit(solution)/shard_map/all_gather | solution.py:89
  12.1 1453.3 %all-gather.3.cloned.1.call-start = ((), (), s32[]{:S(2)}) async-start(), calls=%async_computation | async-start | bytes 8421376 | tf_op jit(solution)/shard_map/all_gather | solution.py:90
  13.6 19.1 %copy-start.5 = (bf16[8,4,512]{2,1,0:T(4,128)(2,1)S(1)}, bf16[8,4,512]{2,1,0:T(4,128)(2,1)}, u32[]{:S(2)}) copy-start(bf16[8,4,512]{2,1,0:T(4,128)(2,1)} %param.11) | copy-start | bytes 98308
  13.6 19.1 %copy-start.7 = (f32[512]{0:T(512)S(1)}, f32[512]{0:T(512)}, u32[]{:S(2)}) copy-start(f32[512]{0:T(512)} %param.14) | copy-start | bytes 6148
  13.6 19.2 %copy-start.4 = (bf16[512,512]{1,0:T(8,128)(2,1)S(1)}, bf16[512,512]{1,0:T(8,128)(2,1)}, u32[]{:S(2)}) copy-start(bf16[512,512]{1,0:T(8,128)(2,1)} %param.16) | copy-start | bytes 1572868
  20.6 4.5 collective-permute-start.1
  21.3 3.7 collective-permute-start
  25.1 7.9 collective-permute-start.3
  27.0 7.6 collective-permute-start.2
  36.4 1.1 copy-start.8
  36.4 1.1 copy-start.9
  46.8 5.5 collective-permute-start.5
  48.4 3.9 collective-permute-start.4
  52.4 8.8 collective-permute-start.7
  59.0 5.7 collective-permute-start.6
  1477.0 7.1 copy-start.3
  1477.0 7.9 copy-start.6
  1484.0 1.6 copy-start.2
  1485.6 6.7 copy-start.1
Sparse Core Ops, SparseCore 0:
  12.2 728.9 all-gather.4
  743.6 721.7 all-gather.2
where the time goes:
time: 1500 us
  waiting for transfers between devices  1380 us (92%)
  local copies, waits for them, and re-layouts  37 us (2%)
  matrix products  27 us (2%)
  starting transfers between devices  23 us (2%)
  other arithmetic  18.8 us (1%)
    all_gather x1, waiting for transfers between devices, local(): lax.all_gather(value_rows, ('lon', 'lat'), axis=0, tiled=True)  705 us
    all_gather x1, waiting for transfers between devices, local(): lax.all_gather(key_rows, ('lon', 'lat'), axis=0, tiled=True)  665 us
  transfers between devices with their start and end apart: 10, of which 6 were waited for; matrix products, arithmetic and copies ran while one was open for 3% of the time, Pallas kernels for 0%

commit v1 on v0

--- a/solution.py
+++ b/solution.py
@@ -86,7 +86,10 @@
     )
     value_rows = projected[:, width_all:].astype(jnp.bfloat16)
     key_rows, value_rows = (key_rows, value_rows)
-    accumulate_key_rows = lax.all_gather(key_rows, ("lon", "lat"), axis=0, tiled=True)
+    known = jax.lax.all_to_all(
+        jnp.stack([key_rows] * jax.lax.psum(1, ("lon", "lat")), axis=0), ("lon", "lat"), 0, 0
+    )
+    accumulate_key_rows = jnp.concatenate(known, axis=0)
     accumulate_value_rows = lax.all_gather(value_rows, ("lon", "lat"), axis=0, tiled=True)
     key_heads = accumulate_key_rows.reshape(accumulate_key_rows.shape[0], head_count, head_size)
     value_heads = accumulate_value_rows.reshape(

time: 1500 us -> 836 us (0.56)
  waiting for transfers between devices: 1380 us -> 678 us
    all_gather x1 -> x0, waiting for transfers between devices: 665 us -> none  [local(): lax.all_gather(key_rows, ('lon', 'lat'), axis=0, tiled=True)]
    all_gather x1, waiting for transfers between devices: 705 us -> 496 us  [local(): lax.all_gather(value_rows, ('lon', 'lat'), axis=0, tiled=True)]
    ppermute x4, waiting for transfers between devices: 5.11 us -> 165 us  [padded_2(): lax.ppermute(lax.slice_in_dim(block, block.shape[dim] - width, None, axis...]
    another operation x0 -> x2, local copies, waits for them, and re-layouts: none -> 25.5 us  [the longest x1 21.2 us: local(): accumulate_key_rows.reshape(accumulate_key_rows.shape[0], head_count, hea...]
    all_to_all x0 -> x1, starting transfers between devices: none -> 15.3 us  [local(): jax.lax.all_to_all(jnp.stack([key_rows] * jax.lax.psum(1, ('lon', 'lat'))...]
  transfers between devices with their start and end apart: 10 -> 10, of which waited for: 6 -> 8; matrix products, arithmetic and copies ran while one was open for 3% -> 8% of each run, Pallas kernels for 0% -> 0%
where the time goes in v1:
time: 836 us; the launch traced here: 830 us
  waiting for transfers between devices  678 us (81%)
  local copies, waits for them, and re-layouts  50 us (6%)
  starting transfers between devices  37.6 us (4%)
  matrix products  33.6 us (4%)
  other arithmetic  16.5 us (2%)
  between operations  14.7 us (2%)
    all_gather x1, waiting for transfers between devices, local(): lax.all_gather(value_rows, ('lon', 'lat'), axis=0, tiled=True)  496 us
    ppermute x4, waiting for transfers between devices, padded_2(): lax.ppermute(lax.slice_in_dim(block, block.shape[dim] - width, None, axis...  165 us
    another operation x1, local copies, waits for them, and re-layouts, local(): accumulate_key_rows.reshape(accumulate_key_rows.shape[0], head_count, hea...  21.2 us
    ppermute x4, waiting for transfers between devices, padded_2(): lax.ppermute(lax.slice_in_dim(block, 0, width, axis=dim), axis, backward)  17 us
  transfers between devices with their start and end apart: 10, of which 8 were waited for; matrix products, arithmetic and copies ran while one was open for 8% of the time, Pallas kernels for 0%

profile of v1, /device:TPU:99, one launch (start us, length us, event | category | flops | bytes accessed | tf_op | source)
XLA Modules:
  0.0 830.2 jit_solution(5702003983773579740)
XLA Ops:
  7.2 0.9 reshape.110
  8.0 0.9 multiply_reduce_fusion.2
  9.0 1.0 fusion.56
  10.6 0.8 slice_bitcast_fusion.3
  11.4 4.3 stack.3
  15.7 15.3 %all-to-all-start = ((bf16[256,32,512]{2,1,0:T(8,128)(2,1)}), bf16[256,32,512]{2,1,0:T(8,128)(2,1)}, u32[]{:S(2)}, u32[]{:S(2)}) async-start(bf16[256,32,512]{2,1,0:T(8,128)(2,1)} %stack.3), calls=%async_computation | async-start | bytes 16777216 | tf_op jit(solution)/shard_map/all_to_all | solution.py:89
  31.1 0.6 slice.102
  31.8 1.8 fusion.7
  33.6 3.4 fusion.14
  37.2 1.3 collective-permute-start
  38.5 162.9 %collective-permute-done = bf16[1,64,128]{2,0,1:T(2,128)(2,1)S(1)} collective-permute-done((bf16[1,64,128]{2,0,1:T(2,128)(2,1)S(1)}, bf16[1,64,128]{2,0,1:T(2,128)(2,1)S(1)}, u32[]{:S(2)}, u32[]{:S(2)}) %collective-permute-start) | collective-permute-done | bytes 16416 | tf_op jit(solution)/shard_map/ppermute | solution.py:15
  201.4 9.5 %collective-permute-done.1 = bf16[1,64,128]{2,0,1:T(2,128)(2,1)S(1)} collective-permute-done((bf16[1,64,128]{2,0,1:T(2,128)(2,1)S(1)}, bf16[1,64,128]{2,0,1:T(2,128)(2,1)S(1)}, u32[]{:S(2)}, u32[]{:S(2)}) %collective-permute-start.1) | collective-permute-done | bytes 16416 | tf_op jit(solution)/shard_map/ppermute | solution.py:18
  210.9 5.8 collective-permute-start.2
  216.7 2.4 collective-permute-start.3
  219.2 0.2 copy.52
  219.5 1.4 collective-permute-done.2
  220.9 3.4 collective-permute-done.3
  224.3 1.7 maximum_bitcast_fusion
  226.1 0.2 pad
  226.3 0.3 copy.46
  226.8 0.4 copy-done.10
  227.2 5.7 broadcast_select_fusion.1
  232.8 0.9 copy.47
  233.8 1.2 multiply_reduce_fusion
  234.9 1.5 multiply_convert_fusion
  236.5 0.3 collective-permute-start.4
  236.8 0.2 collective-permute-start.5
  237.1 0.4 multiply_reduce_fusion.1
  237.5 0.3 collective-permute-done.4
  237.9 3.2 collective-permute-done.5
  241.1 1.9 collective-permute-start.6
  243.0 10.3 %collective-permute-start.7 = (bf16[130,1,128]{2,0,1:T(8,128)(2,1)S(1)}, bf16[130,1,128]{2,0,1:T(8,128)(2,1)S(1)}, u32[]{:S(2)}, u32[]{:S(2)}) collective-permute-start(bf16[130,1,128]{2,0,1:T(8,128)(2,1)S(1)} %get-tuple-element.9), channel_id=1, source_target_pairs={{1,0},{2,1},{3,2},{4,3},{5,4},{6,5},{7,6},{8,7},{9,8},{10,9},{11,1... | collective-permute-start | bytes 99848 | tf_op jit(solution)/shard_map/ppermute | solution.py:18
  253.3 0.8 collective-permute-done.7
  254.2 1.8 maximum_bitcast_fusion.1
  255.9 0.2 pad.2
  256.1 0.3 copy.49
  256.6 5.7 broadcast_select_fusion
  262.3 3.1 copy.50
  265.3 21.2 %reshape_reshape.3 = bf16[8192,8,64]{2,1,0:T(8,128)(2,1)} reshape(bf16[256,32,512]{2,1,0:T(8,128)(2,1)} %all-to-all-done) | data formatting | bytes 16777216 | tf_op jit(solution)/shard_map/reshape;reshape | solution.py:94
  286.6 13.6 %fusion.68 = (f32[8,32]{1,0:T(8,128)S(1)}, bf16[8,32,8192]{2,1,0:T(8,128)(2,1)}) fusion(bf16[8192,8,64]{2,1,0:T(8,128)(2,1)} %reshape_reshape.3, f32[32,8,64]{2,0,1:T(8,128)S(1)} %get-tuple-element.21, f32[64]{0:T(128)S(1)} %get-tuple-element.18, f32[32,8]{0,1:T(8,128)S(1)} %add_rsqrt_fusion.3), kind=kOutput, calls=%fused_computation.90 | convolution fusion | flops 272695040 | bytes 12650752 | tf_op jit(solution)/shard_map/thd,shd->hts/dot_general | solution.py:98
  300.2 496.1 %all-gather.2.cloned.1.call-done = bf16[8192,512]{1,0:T(8,128)(2,1)} async-done(((bf16[32,512]{1,0:T(8,128)(2,1)}), bf16[8192,512]{1,0:T(8,128)(2,1)}) %all-gather.2.cloned.1.call-update) | async-done | bytes 8388624 | tf_op jit(solution)/shard_map/all_gather | solution.py:93
  796.3 11.6 %copy.51 = bf16[8192,512]{0,1:T(8,128)(2,1)} copy(bf16[8192,512]{1,0:T(8,128)(2,1)} %all-gather.2.cloned.1.call-done) | data formatting | bytes 16777216 | tf_op jit(solution)/shard_map/all_gather | solution.py:93
  807.9 6.9 fusion.46
  815.0 0.2 fusion.42
  815.2 0.6 reshape.95
  816.0 0.5 add.82
  816.5 4.0 fusion.16
  820.5 2.7 copy.58
  (57 shorter events, 1.8 us)
Async XLA Ops:
  7.2 1.8 copy-start
  15.7 16.0 %copy-start.9 = (f32[2,128]{1,0:T(2,128)S(1)}, f32[2,128]{1,0:T(2,128)}, u32[]{:S(2)}) copy-start(f32[2,128]{1,0:T(2,128)} %param.12) | copy-start | bytes 3076
  15.7 16.1 %copy-start.2 = (bf16[128,64,128]{2,1,0:T(8,128)(2,1)S(1)}, bf16[128,64,128]{2,1,0:T(8,128)(2,1)}, u32[]{:S(2)}) copy-start(bf16[128,64,128]{2,1,0:T(8,128)(2,1)} %param.10) | copy-start | bytes 6291460
  15.7 249.6 %all-to-all-start = ((bf16[256,32,512]{2,1,0:T(8,128)(2,1)}), bf16[256,32,512]{2,1,0:T(8,128)(2,1)}, u32[]{:S(2)}, u32[]{:S(2)}) async-start(bf16[256,32,512]{2,1,0:T(8,128)(2,1)} %stack.3), calls=%async_computation | async-start | bytes 16777216 | tf_op jit(solution)/shard_map/all_to_all | solution.py:89
  31.0 765.3 %all-gather.2.cloned.1.call-start = ((), (), s32[]{:S(2)}) async-start(), calls=%async_computation.1 | async-start | bytes 8421376 | tf_op jit(solution)/shard_map/all_gather | solution.py:93
  31.8 187.3 %copy-start.6 = (bf16[8,4,512]{2,1,0:T(4,128)(2,1)S(1)}, bf16[8,4,512]{2,1,0:T(4,128)(2,1)}, u32[]{:S(2)}) copy-start(bf16[8,4,512]{2,1,0:T(4,128)(2,1)} %param.11) | copy-start | bytes 98308
  31.8 187.3 %copy-start.8 = (f32[512]{0:T(512)S(1)}, f32[512]{0:T(512)}, u32[]{:S(2)}) copy-start(f32[512]{0:T(512)} %param.14) | copy-start | bytes 6148
  31.8 187.4 %copy-start.5 = (bf16[512,512]{1,0:T(8,128)(2,1)S(1)}, bf16[512,512]{1,0:T(8,128)(2,1)}, u32[]{:S(2)}) copy-start(bf16[512,512]{1,0:T(8,128)(2,1)} %param.16) | copy-start | bytes 1572868
  37.2 164.2 %collective-permute-start = (bf16[1,64,128]{2,0,1:T(2,128)(2,1)S(1)}, bf16[1,64,128]{2,0,1:T(2,128)(2,1)S(1)}, u32[]{:S(2)}, u32[]{:S(2)}) collective-permute-start(bf16[1,64,128]{2,0,1:T(2,128)(2,1)S(1)} %get-tuple-element.14), channel_id=1, source_target_pairs={{0,16},{16,32},{32,48},{48,64},{64,80},{80,96},{96,112},{112,128},... | collective-permute-start | bytes 49160 | tf_op jit(solution)/shard_map/ppermute | solution.py:15
  38.5 172.4 %collective-permute-start.1 = (bf16[1,64,128]{2,0,1:T(2,128)(2,1)S(1)}, bf16[1,64,128]{2,0,1:T(2,128)(2,1)S(1)}, u32[]{:S(2)}, u32[]{:S(2)}) collective-permute-start(bf16[1,64,128]{2,0,1:T(2,128)(2,1)S(1)} %get-tuple-element.15), channel_id=1, source_target_pairs={{16,0},{32,16},{48,32},{64,48},{80,64},{96,80},{112,96},{128,112},... | collective-permute-start | bytes 49160 | tf_op jit(solution)/shard_map/ppermute | solution.py:18
  210.9 10.0 %collective-permute-start.2 = (bf16[130,1,128]{2,0,1:T(8,128)(2,1)S(1)}, bf16[130,1,128]{2,0,1:T(8,128)(2,1)S(1)}, u32[]{:S(2)}, u32[]{:S(2)}) collective-permute-start(bf16[130,1,128]{2,0,1:T(8,128)(2,1)S(1)} %get-tuple-element.10), channel_id=1, source_target_pairs={{0,1},{1,2},{2,3},{3,4},{4,5},{5,6},{6,7},{7,8},{8,9},{9,10},{10,1... | collective-permute-start | bytes 99848 | tf_op jit(solution)/shard_map/ppermute | solution.py:15
  216.7 7.6 collective-permute-start.3
  226.1 1.1 copy-start.10
  226.1 1.1 copy-start.11
  236.5 1.4 collective-permute-start.4
  236.8 4.2 collective-permute-start.5
  241.1 12.2 %collective-permute-start.6 = (bf16[130,1,128]{2,0,1:T(8,128)(2,1)S(1)}, bf16[130,1,128]{2,0,1:T(8,128)(2,1)S(1)}, u32[]{:S(2)}, u32[]{:S(2)}) collective-permute-start(bf16[130,1,128]{2,0,1:T(8,128)(2,1)S(1)} %get-tuple-element.8), channel_id=1, source_target_pairs={{0,1},{1,2},{2,3},{3,4},{4,5},{5,6},{6,7},{7,8},{8,9},{9,10},{10,1... | collective-permute-start | bytes 99848 | tf_op jit(solution)/shard_map/ppermute | solution.py:15
  243.0 11.1 %collective-permute-start.7 = (bf16[130,1,128]{2,0,1:T(8,128)(2,1)S(1)}, bf16[130,1,128]{2,0,1:T(8,128)(2,1)S(1)}, u32[]{:S(2)}, u32[]{:S(2)}) collective-permute-start(bf16[130,1,128]{2,0,1:T(8,128)(2,1)S(1)} %get-tuple-element.9), channel_id=1, source_target_pairs={{1,0},{2,1},{3,2},{4,3},{5,4},{6,5},{7,6},{8,7},{9,8},{10,9},{11,1... | collective-permute-start | bytes 99848 | tf_op jit(solution)/shard_map/ppermute | solution.py:18
  807.9 7.1 copy-start.4
  807.9 7.9 copy-start.7
  814.8 1.6 copy-start.3
  816.5 6.7 copy-start.1
Sparse Core Ops, SparseCore 0:
  34.3 761.9 all-gather.1
